TPU v7x, 512 devices: a whole 4x8x8 slice. The times are simulated.
512 devices in a mesh: samp: 32 (over x, z), blk: 16 (over y, core).
Axes of the slice: x: 4, y: 8, z: 8, core: 2. Of those that a mesh axis runs over, the one named last changes fastest.
Arguments:
- dosages: int32 [49152, 8192], P('samp', 'blk'), may hold values from 0 to 2, as said below
- new_dosages: int32 [49152, 2048], P('samp', 'blk'), may hold values from 0 to 2, as said below
- traits: float32 [64, 49152], P(None, 'samp'), may hold values from -40 to 40
- shrink: float32 [5], replicated, may hold values from 0.5 to 5
Outputs:
- residual: float32 [5, 64, 49152], P(None, 'blk', 'samp')
- scores: float32 [5, 64, 2048], P(None, None, 'blk')
Inputs may be any that keep to these rules, and one draw needn't show every extreme that they name: `dosages`: codes of haplotype pairs, with linkage along neighbouring variants. `new_dosages`: codes of haplotype pairs, with linkage along neighbouring variants.
All inputs are finite; a program needn't handle non-finite values.
Results may differ from a plain program's by a relative error of at most 0.0053.
Values may be sent and summed in bfloat16 or wider, within the bound.
No kernel may reach another device: no remote copies, remote signals or barrier semaphores. Data moves between devices by JAX's collectives and lax.ppermute only.
A program may use at most 64 MiB of HBM per device.

v0:
```python
import jax
import jax.numpy as jnp
from jax import lax
from jax.sharding import PartitionSpec as P

RIDGE = 5
CHEB = 3


def chebyshev(rhs_cols, apply_fn, centre, half_width, sweeps):
    sig_ratio = centre / half_width
    factor = 1.0 / sig_ratio
    direction = rhs_cols / centre
    iterate = jnp.zeros_like(rhs_cols)
    remain = rhs_cols
    for sweep_index in range(sweeps):
        iterate = iterate + direction
        if sweep_index + 1 < sweeps:
            remain = remain - apply_fn(direction)
            factor_next = 1.0 / (2.0 * sig_ratio - factor)
            direction = factor_next * factor * direction + 2.0 * factor_next / half_width * remain
            factor = factor_next
    return iterate


def scaled(values, column_sum, column_sq, count):
    column_mean = column_sum / count
    column_var = column_sq / count - column_mean * column_mean
    inverse = 1.0 / jnp.sqrt(column_var + 1e-05)
    return ((values - column_mean) * inverse).astype(jnp.bfloat16)


def shards(dosages, new_dosages, traits, shrink):
    local_rows = dosages.shape[0]
    trait_count = traits.shape[0]
    count = float(local_rows * lax.axis_size("samp"))
    block_codes = dosages.astype(jnp.float32)
    new_codes = new_dosages.astype(jnp.float32)
    block_sum, block_sq, new_sum, new_sq = lax.psum(
        (
            jnp.sum(block_codes, axis=0),
            jnp.sum(block_codes * block_codes, axis=0),
            jnp.sum(new_codes, axis=0),
            jnp.sum(new_codes * new_codes, axis=0),
        ),
        "samp",
    )
    standard = scaled(block_codes, block_sum, block_sq, count)
    fresh = scaled(new_codes, new_sum, new_sq, count)
    trait_bf = traits.astype(jnp.bfloat16)
    gram = lax.dot_general(
        standard, standard, (((0,), (0,)), ((), ())), preferred_element_type=jnp.float32
    )
    cross = lax.dot_general(
        standard, trait_bf, (((0,), (1,)), ((), ())), preferred_element_type=jnp.float32
    )
    lam_cols = jnp.repeat(shrink, trait_count)
    gram_full, cross_full = lax.psum((gram, cross), "samp")
    bound = jnp.max(jnp.sum(jnp.abs(gram_full), axis=0)) / count

    def apply_full(direction):
        return (
            jnp.dot(gram_full, direction, precision=lax.Precision.HIGHEST) / count
            + lam_cols * direction
        )

    rhs_cols = jnp.tile(cross_full / count, (1, RIDGE))
    weights = chebyshev(
        rhs_cols, apply_full, lam_cols + bound / 2.0, bound / 2.0 + jnp.zeros_like(lam_cols), CHEB
    )
    weight_bf = weights.astype(jnp.bfloat16)
    pred = lax.dot_general(
        weight_bf, standard, (((0,), (1,)), ((), ())), preferred_element_type=jnp.float32
    )
    pred = pred.reshape(RIDGE, trait_count, local_rows)
    share = trait_count // lax.axis_size("blk")
    pred_part = lax.psum_scatter(pred, "blk", scatter_dimension=1, tiled=True)
    own_traits = lax.dynamic_slice_in_dim(traits, lax.axis_index("blk") * share, share, 0)
    residual = own_traits[None, :, :] - pred_part
    res_bf = lax.all_gather(residual.astype(jnp.bfloat16), "blk", axis=1, tiled=True)
    res_flat = res_bf.reshape(RIDGE * trait_count, local_rows)
    raw_part = jnp.dot(res_flat, fresh, preferred_element_type=jnp.float32)
    res_float = res_flat.astype(jnp.float32)
    raw, sum_sq = lax.psum((raw_part, jnp.sum(res_float * res_float, axis=1)), "samp")
    scores = raw / jnp.sqrt(count * (sum_sq / count + 1e-05))[:, None]
    return (residual, scores.reshape(RIDGE, trait_count, fresh.shape[1]))


def solution(mesh):
    placed = (P("samp", "blk"), P("samp", "blk"), P(None, "samp"), P())
    return jax.shard_map(
        shards,
        mesh=mesh,
        in_specs=placed,
        out_specs=(P(None, "blk", "samp"), P(None, None, "blk")),
        check_vma=False,
    )
```

profile of v0, /device:TPU:8, one launch (start us, length us, event | category | flops | bytes accessed | tf_op | source)
XLA Modules:
  0.0 635.6 jit_solution(12466145692508958539)
XLA Ops:
  7.2 0.0 all-reduce.12.cloned.1.call-start
  7.2 2.4 convert_reduce_fusion
  9.6 80.8 %all-reduce.2 = (f32[512]{0:T(512)S(1)}, f32[512]{0:T(512)S(1)}) all-reduce(f32[512]{0:T(512)S(1)} %get-tuple-element.3, f32[512]{0:T(512)S(1)} %get-tuple-element.2), channel_id=1, replica_groups=mesh['samp'=32,'blk'=16] {'samp'}, use_global_device_ids=true, to_apply=%region_3.0 | all-reduce | flops 1024 | bytes 8192 | tf_op jit(solution)/shard_map/psum | solution.py:39
  90.4 2.3 multiply_convert_fusion
  92.8 2.0 fusion.21
  94.8 1.0 fusion.16
  95.9 0.0 all-reduce.10.cloned.1.call-start
  96.0 0.1 broadcast_in_dim.2
  96.0 0.1 reshape.58
  96.1 156.1 %all-reduce.12.cloned.1.call-done = (f32[512,64]{0,1:T(8,128)}, f32[512,512]{1,0:T(8,128)}) async-done(((f32[512,64]{0,1:T(8,128)}, f32[512,512]{1,0:T(8,128)}), (f32[512,64]{0,1:T(8,128)}, f32[512,512]{1,0:T(8,128)})) %all-reduce.12.cloned.1.call-update) | async-done | bytes 1179664 | tf_op jit(solution)/shard_map/psum | solution.py:58
  252.2 1.5 abs_reduce_fusion
  253.7 0.6 reduce_max.9
  255.0 0.9 broadcast_multiply_fusion
  255.9 0.1 bitcast_divide_fusion
  256.0 0.1 tile.4
  256.1 1.3 fusion.6
  257.4 1.6 fusion.7
  259.1 2.0 fusion.22
  261.1 0.0 all-reduce.8.cloned.1.call-start
  261.2 1.3 dynamic-slice
  263.1 0.2 convert_reduce_fusion.1
  263.4 113.1 %all-reduce.10.cloned.1.call-done = f32[5,64,1536]{2,1,0:T(8,128)} async-done(((f32[5,64,1536]{2,1,0:T(8,128)}), f32[5,64,1536]{2,1,0:T(8,128)}) %all-reduce.10.cloned.1.call-update) | async-done | bytes 1966096
  376.5 1.6 fusion.20
  378.1 21.2 %all_gather.3 = bf16[5,64,1536]{2,0,1:T(8,128)(2,1)S(1)} all-gather(bf16[5,4,1536]{2,0,1:T(8,128)(2,1)S(1)} %copy.11), channel_id=1, replica_groups=mesh['samp'=32,'blk'=16] {'blk'}, dimensions={1}, use_global_device_ids=true | all-gather | bytes 1044480 | tf_op jit(solution)/shard_map/all_gather | solution.py:80
  399.4 0.5 multiply_reduce_fusion
  399.9 0.3 copy.12
  400.2 0.1 copy.13
  400.3 0.1 reduce_sum.62
  400.4 75.6 %all-reduce.1 = (f32[128]{0:T(128)S(1)}, f32[128]{0:T(128)S(1)}, f32[320]{0:T(512)S(1)}) all-reduce(f32[128]{0:T(128)S(1)} %get-tuple-element.5, f32[128]{0:T(128)S(1)} %get-tuple-element.4, f32[320]{0:T(512)S(1)} %reduce_sum.62), channel_id=1, replica_groups=mesh['samp'=32,'blk'=16] {'samp'}, use_global_device_ids=true, to_apply=%region_12.0 | all-reduce | flops 576 | bytes 4608 | tf_op jit(solution)/shard_map/psum | solution.py:39
  476.0 1.1 fusion.11
  477.1 150.2 %all-reduce.8.cloned.1.call-done = f32[320,128]{1,0:T(8,128)} async-done(((f32[320,128]{1,0:T(8,128)}), f32[320,128]{1,0:T(8,128)}) %all-reduce.8.cloned.1.call-update) | async-done | bytes 163856 | tf_op jit(solution)/shard_map/psum | solution.py:84
  627.4 1.7 broadcast_divide_fusion
  (18 shorter events, 0.1 us)
Async XLA Ops:
  7.2 245.0 %all-reduce.12.cloned.1.call-start = ((), (), s32[]{:S(2)}) async-start(), calls=%async_computation.2 | async-start | bytes 2359296 | tf_op jit(solution)/shard_map/psum | solution.py:58
  92.8 2.1 copy-start.2
  94.8 1.1 copy-start.3
  95.9 280.6 %all-reduce.10.cloned.1.call-start = ((), (), s32[]{:S(2)}) async-start(), calls=%async_computation.1 | async-start | bytes 3932160
  252.2 3.9 copy-start
  261.1 2.1 copy-start.1
  261.1 366.3 %all-reduce.8.cloned.1.call-start = ((), (), s32[]{:S(2)}) async-start(), calls=%async_computation | async-start | bytes 327680 | tf_op jit(solution)/shard_map/psum | solution.py:84
Sparse Core Ops, SparseCore 0:
  96.0 156.1 all-reduce.11
  261.2 115.2 all-reduce.9
  477.2 150.0 all-reduce.7
where the time goes:
time: 636 us
  waiting for transfers between devices  419 us (66%)
  blocking collectives  178 us (28%)
  between operations  15.2 us (2%)
  other arithmetic  11.9 us (2%)
  matrix products  9.16 us (1%)
    psum x2, blocking collectives, shards(): lax.psum((jnp.sum(block_codes, axis=0), jnp.sum(block_codes * block_codes...  156 us
    psum x1, waiting for transfers between devices, shards(): gram_full, cross_full = lax.psum((gram, cross), 'samp')  156 us
    psum x1, waiting for transfers between devices, shards(): lax.psum((raw_part, jnp.sum(res_float * res_float, axis=1)), 'samp')  150 us
    unnamed x4, waiting for transfers between devices  113 us
    all_gather x1, blocking collectives, shards(): lax.all_gather(residual.astype(jnp.bfloat16), 'blk', axis=1, tiled=True)  21.2 us
  transfers between devices with their start and end apart: 3, of which 3 were waited for; matrix products, arithmetic and copies ran while one was open for 0% of the time, Pallas kernels for 0%

commit v1 on v0

--- a/solution.py
+++ b/solution.py
@@ -77,7 +77,9 @@
     pred_part = lax.psum_scatter(pred, "blk", scatter_dimension=1, tiled=True)
     own_traits = lax.dynamic_slice_in_dim(traits, lax.axis_index("blk") * share, share, 0)
     residual = own_traits[None, :, :] - pred_part
-    res_bf = lax.all_gather(residual.astype(jnp.bfloat16), "blk", axis=1, tiled=True)
+    block = residual.astype(jnp.bfloat16)
+    sent = jnp.stack([block] * lax.axis_size("blk"))
+    res_bf = jnp.concatenate(lax.all_to_all(sent, "blk", 0, 0), axis=1)
     res_flat = res_bf.reshape(RIDGE * trait_count, local_rows)
     raw_part = jnp.dot(res_flat, fresh, preferred_element_type=jnp.float32)
     res_float = res_flat.astype(jnp.float32)

time: 636 us -> 647 us (1.017)
  waiting for transfers between devices: 419 us -> 441 us
  blocking collectives: 178 us -> 157 us
  starting transfers between devices: 0.12 us -> 8.66 us
    all_to_all x0 -> x1, waiting for transfers between devices: none -> 22.9 us  [shards(): res_bf = jnp.concatenate(lax.all_to_all(sent, 'blk', 0, 0), axis=1)]
    all_gather x1 -> x0, blocking collectives: 21.2 us -> none  [shards(): lax.all_gather(residual.astype(jnp.bfloat16), 'blk', axis=1, tiled=True)]
    all_to_all x0 -> x1, starting transfers between devices: none -> 8.55 us  [shards(): res_bf = jnp.concatenate(lax.all_to_all(sent, 'blk', 0, 0), axis=1)]
  transfers between devices with their start and end apart: 3 -> 4, of which waited for: 3 -> 4; matrix products, arithmetic and copies ran while one was open for 0% -> 0% of each run, Pallas kernels for 0% -> 0%
where the time goes in v1:
time: 647 us; the launch traced here: 646 us
  waiting for transfers between devices  441 us (68%)
  blocking collectives  157 us (24%)
  between operations  15.2 us (2%)
  other arithmetic  12 us (2%)
  matrix products  9.16 us (1%)
  starting transfers between devices  8.66 us (1%)
    psum x2, blocking collectives, shards(): lax.psum((jnp.sum(block_codes, axis=0), jnp.sum(block_codes * block_codes...  157 us
    psum x1, waiting for transfers between devices, shards(): gram_full, cross_full = lax.psum((gram, cross), 'samp')  156 us
    psum x1, waiting for transfers between devices, shards(): lax.psum((raw_part, jnp.sum(res_float * res_float, axis=1)), 'samp')  149 us
    unnamed x4, waiting for transfers between devices  113 us
    all_to_all x1, waiting for transfers between devices, shards(): res_bf = jnp.concatenate(lax.all_to_all(sent, 'blk', 0, 0), axis=1)  22.9 us
  transfers between devices with their start and end apart: 4, of which 4 were waited for; matrix products, arithmetic and copies ran while one was open for 0% of the time, Pallas kernels for 0%

profile of v1, /device:TPU:8, one launch (start us, length us, event | category | flops | bytes accessed | tf_op | source)
XLA Modules:
  0.0 646.1 jit_solution(5539306916869710371)
XLA Ops:
  7.2 2.4 convert_reduce_fusion
  9.6 80.8 %all-reduce.2 = (f32[512]{0:T(512)S(1)}, f32[512]{0:T(512)S(1)}) all-reduce(f32[512]{0:T(512)S(1)} %get-tuple-element.3, f32[512]{0:T(512)S(1)} %get-tuple-element.2), channel_id=1, replica_groups=mesh['samp'=32,'blk'=16] {'samp'}, use_global_device_ids=true, to_apply=%region_3.0 | all-reduce | flops 1024 | bytes 8192 | tf_op jit(solution)/shard_map/psum | solution.py:39
  90.4 2.3 multiply_convert_fusion
  92.8 2.0 fusion.21
  94.8 1.0 fusion.16
  95.9 0.0 all-reduce.10.cloned.1.call-start
  96.0 0.1 broadcast_in_dim.2
  96.0 0.1 reshape.60
  96.1 156.1 %all-reduce.12.cloned.1.call-done = (f32[512,64]{0,1:T(8,128)}, f32[512,512]{1,0:T(8,128)}) async-done(((f32[512,64]{0,1:T(8,128)}, f32[512,512]{1,0:T(8,128)}), (f32[512,64]{0,1:T(8,128)}, f32[512,512]{1,0:T(8,128)})) %all-reduce.12.cloned.1.call-update) | async-done | bytes 1179664 | tf_op jit(solution)/shard_map/psum | solution.py:58
  252.2 1.5 abs_reduce_fusion
  253.7 0.6 reduce_max.9
  255.0 0.9 broadcast_multiply_fusion
  255.9 0.1 bitcast_divide_fusion
  256.0 0.1 tile.4
  256.1 1.3 fusion.6
  257.4 1.6 fusion.7
  259.1 2.0 fusion.22
  261.1 1.3 dynamic-slice
  263.1 113.3 %all-reduce.10.cloned.1.call-done = f32[5,64,1536]{2,1,0:T(8,128)} async-done(((f32[5,64,1536]{2,1,0:T(8,128)}), f32[5,64,1536]{2,1,0:T(8,128)}) %all-reduce.10.cloned.1.call-update) | async-done | bytes 1966096
  376.5 1.6 fusion.20
  378.1 1.2 stack.2
  379.3 8.5 %all-to-all-start = ((bf16[16,5,4,1536]{3,2,1,0:T(4,128)(2,1)}), bf16[16,5,4,1536]{3,2,1,0:T(4,128)(2,1)S(1)}, u32[]{:S(2)}, u32[]{:S(2)}) async-start(bf16[16,5,4,1536]{3,2,1,0:T(4,128)(2,1)} %stack.2), calls=%async_computation | async-start | bytes 1966080 | tf_op jit(solution)/shard_map/all_to_all | solution.py:82
  387.9 0.2 convert_reduce_fusion.1
  388.1 22.9 %all-to-all-done = bf16[16,5,4,1536]{3,2,1,0:T(4,128)(2,1)S(1)} async-done(((bf16[16,5,4,1536]{3,2,1,0:T(4,128)(2,1)}), bf16[16,5,4,1536]{3,2,1,0:T(4,128)(2,1)S(1)}, u32[]{:S(2)}, u32[]{:S(2)}) %all-to-all-start) | async-done | bytes 983072 | tf_op jit(solution)/shard_map/all_to_all | solution.py:82
  411.1 0.6 multiply_reduce_fusion.1
  411.7 0.1 reduce_sum.62
  411.8 0.3 copy.7
  412.1 0.2 reshape_reshape.3
  412.4 75.7 %all-reduce.1 = (f32[128]{0:T(128)S(1)}, f32[128]{0:T(128)S(1)}, f32[320]{0:T(512)S(1)}) all-reduce(f32[128]{0:T(128)S(1)} %get-tuple-element.5, f32[128]{0:T(128)S(1)} %get-tuple-element.4, f32[320]{0:T(512)S(1)} %reduce_sum.62), channel_id=1, replica_groups=mesh['samp'=32,'blk'=16] {'samp'}, use_global_device_ids=true, to_apply=%region_12.0 | all-reduce | flops 576 | bytes 4608 | tf_op jit(solution)/shard_map/psum | solution.py:39
  488.1 1.1 fusion.11
  489.2 148.7 %all-reduce.8.cloned.1.call-done = f32[320,128]{1,0:T(8,128)} async-done(((f32[320,128]{1,0:T(8,128)}), f32[320,128]{1,0:T(8,128)}) %all-reduce.8.cloned.1.call-update) | async-done | bytes 163856 | tf_op jit(solution)/shard_map/psum | solution.py:86
  637.9 1.7 broadcast_divide_fusion
  (20 shorter events, 0.2 us)
Async XLA Ops:
  7.2 245.0 %all-reduce.12.cloned.1.call-start = ((), (), s32[]{:S(2)}) async-start(), calls=%async_computation.3 | async-start | bytes 2359296 | tf_op jit(solution)/shard_map/psum | solution.py:58
  92.8 2.1 copy-start.2
  94.8 1.1 copy-start.3
  95.9 280.6 %all-reduce.10.cloned.1.call-start = ((), (), s32[]{:S(2)}) async-start(), calls=%async_computation.2 | async-start | bytes 3932160
  252.2 3.9 copy-start
  261.1 126.8 %copy-start.1 = (s32[1536,128]{1,0:T(8,128)S(1)}, s32[1536,128]{1,0:T(8,128)}, u32[]{:S(2)}) copy-start(s32[1536,128]{1,0:T(8,128)} %param.5) | copy-start | bytes 2359300
  379.3 31.8 %all-to-all-start = ((bf16[16,5,4,1536]{3,2,1,0:T(4,128)(2,1)}), bf16[16,5,4,1536]{3,2,1,0:T(4,128)(2,1)S(1)}, u32[]{:S(2)}, u32[]{:S(2)}) async-start(bf16[16,5,4,1536]{3,2,1,0:T(4,128)(2,1)} %stack.2), calls=%async_computation | async-start | bytes 1966080 | tf_op jit(solution)/shard_map/all_to_all | solution.py:82
  387.9 250.1 %all-reduce.8.cloned.1.call-start = ((), (), s32[]{:S(2)}) async-start(), calls=%async_computation.1 | async-start | bytes 327680 | tf_op jit(solution)/shard_map/psum | solution.py:86
Sparse Core Ops, SparseCore 0:
  96.0 156.1 all-reduce.11
  261.2 115.2 all-reduce.9
  489.3 148.5 all-reduce.7
